TPU v7x, 32 devices: a whole 2x2x4 slice. The times are simulated.
32 devices in a mesh: batch: 4 (over z), neg: 2 (over y), weight: 4 (over x, core).
Axes of the slice: x: 2, y: 2, z: 4, core: 2. Of those that a mesh axis runs over, the one named last changes fastest.
Arguments:
- images: bfloat16 [1024, 2048], P('batch'), may hold values from -30 to 30
- img_pair: int32 [1024], P('batch'), may hold values from 0 to 1023, each once
- texts: bfloat16 [1024, 2048], P(('batch', 'neg', 'weight')), may hold values from -100 to 100
- txt_pair: int32 [1024], P(('batch', 'neg', 'weight')), may hold values from 0 to 1023, each once
- gain: float32 [2048], replicated, may hold values from 0.1 to 1.9
- perm: int32 [2048], replicated, may hold values from 0 to 2047, each once
- right_blocks: bfloat16 [32, 64, 64], P('weight'), may hold values from -0.75 to 0.75
- left_blocks: bfloat16 [32, 64, 64], P('weight'), may hold values from -0.75 to 0.75
Outputs:
- grad_img: bfloat16 [1024, 2048], P(('batch', 'neg', 'weight'))
- row_loss: float32 [1024], P('batch')
Inputs may be any that keep to these rules, and one draw needn't show every extreme that they name: Every pair id appears once in img_pair and once in txt_pair.
All inputs are finite; a program needn't handle non-finite values.
Results may differ from a plain program's by a relative error of at most 0.0065.
Values may be sent and summed in bfloat16 or wider, within the bound.
A program may use at most 64 MiB of HBM per device.

v0:
```python
import math

import jax
import jax.numpy as jnp
from jax import lax
from jax.sharding import PartitionSpec as P

LOGIT_GAIN = 2.8


def monarch(images, gain, perm, right_full, left_full):
    row_count, width = images.shape
    block_count, block_size = (right_full.shape[0], right_full.shape[1])
    values = images.astype(jnp.float32)
    row_mean = jnp.mean(values, axis=1, keepdims=True)
    centered = values - row_mean
    row_var = jnp.mean(centered * centered, axis=1, keepdims=True)
    normed = (centered * lax.rsqrt(row_var + 1e-05) * gain).astype(jnp.bfloat16)
    inner_mixed = jnp.einsum(
        "rke,kec->rkc",
        normed.reshape(row_count, block_count, block_size),
        right_full,
        preferred_element_type=jnp.float32,
    )
    active = (
        jax.nn.gelu(inner_mixed, approximate=True).astype(jnp.bfloat16).reshape(row_count, width)
    )
    permuted = jnp.take(active, perm, axis=1)
    outer_mixed = jnp.einsum(
        "rke,kec->rkc",
        permuted.reshape(row_count, block_count, block_size),
        left_full,
        preferred_element_type=jnp.float32,
    )
    return (values + outer_mixed.reshape(row_count, width)).astype(jnp.bfloat16)


def per_device(images, img_pair, texts, txt_pair, gain, perm, right_blocks, left_blocks):
    right_full, left_full = (
        lax.all_gather(right_blocks, "weight", axis=0, tiled=True),
        lax.all_gather(left_blocks, "weight", axis=0, tiled=True),
    )
    embedded = monarch(images, gain, perm, right_full, left_full)
    gathered, gathered_pair = (
        lax.all_gather(texts, "batch", axis=0, tiled=True),
        lax.all_gather(txt_pair, "batch", axis=0, tiled=True),
    )
    logit_scale = LOGIT_GAIN / math.sqrt(images.shape[1])
    scores = (
        jnp.einsum("rd,cd->rc", embedded, gathered, preferred_element_type=jnp.float32)
        * logit_scale
    )
    matches = (img_pair[:, None] == gathered_pair[None, :]).astype(jnp.float32)
    local_max = jnp.max(scores, axis=1)
    local_pos = jnp.sum(matches * scores, axis=1)
    row_max = lax.pmax(local_max, ("neg", "weight"))
    shifted = jnp.exp(scores - row_max[:, None])
    totals, positive = lax.psum((jnp.sum(shifted, axis=1), local_pos), ("neg", "weight"))
    row_loss = row_max + jnp.log(totals) - positive
    dscore = (shifted / totals[:, None] - matches).astype(jnp.bfloat16)
    grad_sum = lax.psum_scatter(
        jnp.dot(dscore, gathered, preferred_element_type=jnp.float32),
        ("neg", "weight"),
        scatter_dimension=0,
        tiled=True,
    )
    grad_img = grad_sum.astype(jnp.bfloat16)
    return (grad_img, row_loss)


def solution(mesh):
    return jax.shard_map(
        per_device,
        mesh=mesh,
        in_specs=(
            P("batch", None),
            P("batch"),
            P(("batch", "neg", "weight"), None),
            P(("batch", "neg", "weight")),
            P(),
            P(),
            P("weight", None, None),
            P("weight", None, None),
        ),
        out_specs=(P(("batch", "neg", "weight"), None), P("batch")),
        check_vma=False,
    )
```

profile of v0, /device:TPU:0, one launch (start us, length us, event | category | flops | bytes accessed | tf_op | source)
XLA Modules:
  0.0 139.5 jit_solution(6286460170764217933)
XLA Ops:
  7.2 0.0 reduce-scatter.2.cloned.1.call-start
  7.2 0.7 fusion.28
  7.9 0.7 compare_and_fusion
  8.6 0.0 copy-start
  8.6 0.0 copy-start.1
  8.6 1.5 %copy.17 = bf16[256,2048]{0,1:T(8,128)(2,1)S(1)} copy(bf16[256,2048]{1,0:T(8,128)(2,1)} %param.8) | data formatting | bytes 2097152 | tf_op args[0]
  10.2 0.0 copy-start.3
  10.2 0.3 convert_reduce_fusion
  10.5 0.3 fusion.2
  10.8 0.0 copy-done
  10.8 8.6 %all_gather.12 = bf16[32,64,64]{2,1,0:T(8,128)(2,1)S(1)} all-gather(bf16[8,64,64]{2,1,0:T(8,128)(2,1)S(1)} %copy-done), channel_id=1, replica_groups=mesh['batch'=4,'neg'=2,'weight'=4] {'weight'}, dimensions={0}, use_global_device_ids=true | all-gather | bytes 327680 | tf_op jit(solution)/shard_map/all_gather | solution.py:40
  19.5 0.0 copy-done.1
  19.5 7.7 %all_gather.13 = bf16[32,64,64]{2,1,0:T(8,128)(2,1)} all-gather(bf16[8,64,64]{2,1,0:T(8,128)(2,1)S(1)} %copy-done.1), channel_id=1, replica_groups=mesh['batch'=4,'neg'=2,'weight'=4] {'weight'}, dimensions={0}, use_global_device_ids=true | all-gather | bytes 327680 | tf_op jit(solution)/shard_map/all_gather | solution.py:41
  27.2 0.1 broadcast_in_dim.21
  27.3 0.0 copy-done.3
  27.3 0.4 fusion.4
  27.6 0.9 fusion.13
  28.5 7.5 %gather_fusion = bf16[2048,256]{1,0:T(8,128)(2,1)S(1)} fusion(bf16[256,2048]{0,1:T(8,128)(2,1)S(1)} %bitcast.18, s32[2048]{0:T(1024)S(1)} %fusion.28), kind=kCustom, calls=%fused_computation | custom fusion | bytes 2105344 | tf_op jit(solution)/shard_map/jit(_take)/gather | solution.py:28
  36.0 1.9 %fusion.14 = f32[32,256,64]{1,2,0:T(8,128)S(1)} fusion(bf16[32,64,64]{2,1,0:T(8,128)(2,1)} %all_gather.13, bf16[256,32,64]{0,2,1:T(8,128)(2,1)S(1)} %bitcast.19, pred[32,64]{1,0:T(8,128)(4,1)S(1)} %broadcast_in_dim.21), kind=kOutput, calls=%fused_computation.20 | convolution fusion | flops 67633152 | bytes 3409920 | tf_op jit(solution)/shard_map/rke,kec->rkc/dot_general | solution.py:29
  38.0 0.0 copy-start.2
  38.0 0.3 fusion.5
  38.3 0.6 copy-done.2
  38.9 0.0 copy-start.6
  38.9 0.0 copy-start.5
  38.9 0.0 copy-start.4
  38.9 16.5 %all_gather.14 = bf16[128,2048]{1,0:T(8,128)(2,1)S(1)} all-gather(bf16[32,2048]{1,0:T(8,128)(2,1)S(1)} %copy-done.2), channel_id=1, replica_groups=mesh['batch'=4,'neg'=2,'weight'=4] {'batch'}, dimensions={0}, use_global_device_ids=true | all-gather | bytes 655360 | tf_op jit(solution)/shard_map/all_gather | solution.py:45
  55.3 0.3 fusion.30
  55.7 12.3 %pmax.7 = f32[256]{0:T(256)S(1)} all-reduce(f32[256]{0:T(256)S(1)} %get-tuple-element.6), channel_id=1, replica_groups=mesh['batch'=4,'neg'=2,'weight'=4] {'neg','weight'}, use_global_device_ids=true, to_apply=%region_3.4 | all-reduce | flops 256 | bytes 2048 | tf_op jit(solution)/shard_map/pmax | solution.py:56
  68.0 0.0 copy-done.6
  68.0 0.6 dynamic-slice
  69.2 0.0 copy-done.5
  69.2 0.2 dynamic-update-slice
  69.5 7.7 %all-reduce = s32[128]{0:T(128)S(1)} all-reduce(s32[128]{0:T(128)S(1)} %dynamic-update-slice), channel_id=1, replica_groups=mesh['batch'=4,'neg'=2,'weight'=4] {'batch'}, use_global_device_ids=true, to_apply=%add | all-reduce | flops 128 | bytes 1024
  77.1 0.0 copy-done.4
  77.1 0.1 fusion.20
  77.3 11.8 %all-reduce.1 = (f32[256]{0:T(256)S(1)}, f32[256]{0:T(256)S(1)}) all-reduce(f32[256]{0:T(256)S(1)} %get-tuple-element.3, f32[256]{0:T(256)S(1)} %get-tuple-element.2), channel_id=1, replica_groups=mesh['batch'=4,'neg'=2,'weight'=4] {'neg','weight'}, use_global_device_ids=true, to_apply=%region_5.6 | all-reduce | flops 512 | bytes 4096 | tf_op jit(solution)/shard_map/psum | solution.py:58
  89.0 1.9 %fusion.22 = f32[256,2048]{1,0:T(8,128)} fusion(bf16[128,2048]{1,0:T(8,128)(2,1)S(1)} %all_gather.14, f32[256,128]{0,1:T(8,128)S(1)} %get-tuple-element.7, s32[256]{0:T(256)S(1)} %copy-done.4, f32[256]{0:T(256)S(1)} %get-tuple-element.4, f32[256]{0:T(256)S(1)} %pmax.7, s32[128]{0:T(128)S(1)} %all-reduce), kind=kOutput, calls=%fused_computation.31 | convolution fusion | flops 134414336 | bytes 2756096 | tf_op jit(solution)/shard_map/dot_general | solution.py:62
  90.9 0.0 reduce-scatter.2.cloned.1.call-update
  90.9 0.6 add_subtract_fusion
  91.5 39.5 %reduce-scatter.2.cloned.1.call-done = f32[32,2048]{1,0:T(8,128)} async-done(((f32[256,2048]{1,0:T(8,128)}), f32[32,2048]{1,0:T(8,128)}) %reduce-scatter.2.cloned.1.call-update) | async-done | bytes 262160 | tf_op jit(solution)/shard_map/reduce_scatter | solution.py:61
  131.0 1.6 %convert_element_type.27 = bf16[32,2048]{1,0:T(8,128)(2,1)} convert(f32[32,2048]{1,0:T(8,128)} %reduce-scatter.2.cloned.1.call-done) | non-fusion elementwise | flops 65536 | bytes 393216 | tf_op jit(solution)/shard_map/convert_element_type | solution.py:67
  (3 shorter events, 0.0 us)
Async XLA Ops:
  7.2 123.9 %reduce-scatter.2.cloned.1.call-start = ((), (), s32[]{:S(2)}) async-start(), calls=%async_computation.1 | async-start | bytes 2359296 | tf_op jit(solution)/shard_map/reduce_scatter | solution.py:61
  8.6 2.2 %copy-start = (bf16[8,64,64]{2,1,0:T(8,128)(2,1)S(1)}, bf16[8,64,64]{2,1,0:T(8,128)(2,1)}, u32[]{:S(2)}) copy-start(bf16[8,64,64]{2,1,0:T(8,128)(2,1)} %param.14) | copy-start | bytes 196612
  8.6 10.8 %copy-start.1 = (bf16[8,64,64]{2,1,0:T(8,128)(2,1)S(1)}, bf16[8,64,64]{2,1,0:T(8,128)(2,1)}, u32[]{:S(2)}) copy-start(bf16[8,64,64]{2,1,0:T(8,128)(2,1)} %param.15) | copy-start | bytes 196612
  10.2 17.1 %copy-start.3 = (f32[2048]{0:T(1024)S(1)}, f32[2048]{0:T(1024)}, u32[]{:S(2)}) copy-start(f32[2048]{0:T(1024)} %param.12) | copy-start | bytes 24580
  38.0 0.9 copy-start.2
  38.9 29.1 %copy-start.6 = (u32[32]{0:T(128)S(1)}, u32[32]{0:T(128)}, u32[]{:S(2)}) copy-start(u32[32]{0:T(128)} %constant.39) | copy-start | bytes 388
  38.9 30.4 %copy-start.5 = (s32[32]{0:T(128)S(1)}, s32[32]{0:T(128)}, u32[]{:S(2)}) copy-start(s32[32]{0:T(128)} %param.11) | copy-start | bytes 388
  38.9 38.3 %copy-start.4 = (s32[256]{0:T(256)S(1)}, s32[256]{0:T(256)}, u32[]{:S(2)}) copy-start(s32[256]{0:T(256)} %param.9) | copy-start | bytes 3076
Sparse Core Ops, SparseCore 0:
  91.1 39.9 reduce-scatter.1
where the time goes:
time: 140 us
  blocking collectives  64.6 us (46%)
  waiting for transfers between devices  39.5 us (28%)
  between operations  14.8 us (11%)
  local copies, waits for them, and re-layouts  10.6 us (8%)
  matrix products  5.03 us (4%)
  other arithmetic  4.98 us (4%)
    reduce_scatter x1, waiting for transfers between devices, per_device(): lax.psum_scatter(jnp.dot(dscore, gathered, preferred_element_type=jnp.flo...  39.5 us
    all_gather x1, blocking collectives, per_device(): lax.all_gather(texts, 'batch', axis=0, tiled=True)  16.5 us
    pmax x1, blocking collectives, per_device(): row_max = lax.pmax(local_max, ('neg', 'weight'))  12.3 us
    psum x1, blocking collectives, per_device(): lax.psum((jnp.sum(shifted, axis=1), local_pos), ('neg', 'weight'))  11.8 us
    all_gather x1, blocking collectives, per_device(): lax.all_gather(right_blocks, 'weight', axis=0, tiled=True)  8.65 us
    all_gather x1, blocking collectives, per_device(): lax.all_gather(left_blocks, 'weight', axis=0, tiled=True)  7.71 us
    unnamed x1, blocking collectives  7.67 us
    gather x1, local copies, waits for them, and re-layouts, monarch(): permuted = jnp.take(active, perm, axis=1)  7.5 us
  transfers between devices with their start and end apart: 1, of which 1 were waited for; matrix products, arithmetic and copies ran while one was open for 0% of the time, Pallas kernels for 0%

commit v1 on v0

--- a/solution.py
+++ b/solution.py
@@ -1,11 +1,373 @@
+import functools
 import math
 
 import jax
 import jax.numpy as jnp
 from jax import lax
+from jax.experimental import pallas as pl
+from jax.experimental.pallas import tpu as pltpu
 from jax.sharding import PartitionSpec as P
 
 LOGIT_GAIN = 2.8
+MESH = pl.DeviceIdType.MESH
+F32, BF16 = jnp.float32, jnp.bfloat16
+VMEM_FOR_TEXTS = 16 * 2**20
+
+
+def plane_orders(count):
+    return [sorted(range(count), key=lambda o: (abs(o - own), o)) for own in range(count)]
+
+
+def block_diagonal(wide):
+    size = wide.shape[0]
+    lane = lax.broadcasted_iota(jnp.int32, wide.shape, 1)
+    values = wide.astype(F32)
+    upper = jnp.where(lane < size, values, 0.0)
+    lower = jnp.where(lane < size, 0.0, values)
+    return jnp.concatenate([upper, lower], axis=0).astype(BF16)
+
+
+def fused_kernel(
+    dims, images_ref, img_pair_ref, texts_ref, txt_pair_ref, gain_ref, perm_ref, right_ref, left_ref,
+    grad_ref, loss_ref,
+    rows_ref, wts, buf, pairs, normed_ref, active_ref, permuted_ref, emb_ref, score_ref, losses,
+    local_sem, wt_send, wt_recv, send_sem, recv_sem, pair_send, pair_recv, loss_send, loss_recv,
+):
+    nb, nn, nw = dims
+    width = texts_ref.shape[1]
+    t_rows = texts_ref.shape[0]
+    block_count, size = right_ref.shape[0], right_ref.shape[1]
+    pair_count = block_count // 2
+    lanes = 2 * size
+    r_rows = rows_ref.shape[0]
+    group = nn * nw
+    b, n, w = lax.axis_index("batch"), lax.axis_index("neg"), lax.axis_index("weight")
+    core = lax.rem(w, 2)
+    far = 1 - 2 * lax.div(w, 2)
+    flip = 1 - 2 * n
+    n_a, w_a = n + core * flip, w + (1 - core) * 2 * far
+    n_b, w_b = n + (1 - core) * flip, w + core * 2 * far
+    n_d, w_d = 1 - n, w + 2 * far
+    w_p = w + 1 - 2 * core
+    dev_a, dev_b, dev_p = (b, n_a, w_a), (b, n_b, w_b), (b, n, w_p)
+    dev_x = (b, n, w_d)
+    dev_up, dev_down = (b + 1, n, w), (b - 1, n, w)
+    me = n * nw + w
+
+    def slot(o, nn_, ww_):
+        return (o * nn + nn_) * nw + ww_
+
+    orders = plane_orders(nb)
+
+    def origin(k):
+        value = jnp.int32(orders[0][k])
+        for own in range(1, nb):
+            value = jnp.where(b == own, orders[own][k], value)
+        return value
+
+    planes = [origin(k) for k in range(nb)]
+
+    own_slot = slot(b, n, w)
+    copy_rows = pltpu.make_async_copy(images_ref.at[pl.ds(pl.multiple_of(me * r_rows, r_rows), r_rows)], rows_ref, local_sem.at[0])
+    copy_text = pltpu.make_async_copy(texts_ref, buf.at[own_slot], local_sem.at[1])
+    copy_rows.start()
+    copy_text.start()
+    for k in range(pair_count):
+        wts[w, k] = jnp.concatenate([right_ref[2 * k], right_ref[2 * k + 1]], axis=1)
+        wts[w, pair_count + k] = jnp.concatenate([left_ref[2 * k], left_ref[2 * k + 1]], axis=1)
+    ids = txt_pair_ref[...]
+    pairs[own_slot] = jnp.concatenate([ids] * nw, axis=1)
+
+    barrier = pltpu.get_barrier_semaphore()
+    near = [dev_a, dev_b, dev_p, (b, n_d, w_d)]
+    near += [(b, n_a, w_a + 1 - 2 * core), (b, n_b, w_b + 1 - 2 * core), (b, n_d, w_d + 1 - 2 * core)]
+    for dev in near:
+        pl.semaphore_signal(barrier, inc=1, device_id=dev, device_id_type=MESH)
+
+    @pl.when(b < nb - 1)
+    def _():
+        pl.semaphore_signal(barrier, inc=1, device_id=dev_up, device_id_type=MESH)
+
+    @pl.when(b > 0)
+    def _():
+        pl.semaphore_signal(barrier, inc=1, device_id=dev_down, device_id_type=MESH)
+
+    expected = len(near) + jnp.where(b < nb - 1, 1, 0) + jnp.where(b > 0, 1, 0)
+    pl.semaphore_wait(barrier, expected)
+
+    def weight_copy(index, kind, dev):
+        return pltpu.make_async_remote_copy(
+            src_ref=wts.at[index], dst_ref=wts.at[index], send_sem=wt_send.at[kind], recv_sem=wt_recv.at[index],
+            device_id=dev, device_id_type=MESH,
+        )
+
+    weight_copy(w, 0, dev_x).start()
+    weight_copy(w, 1, dev_p).start()
+
+    def text_copy(index, kind, dev, source):
+        return pltpu.make_async_remote_copy(
+            src_ref=source, dst_ref=buf.at[index], send_sem=send_sem.at[index, kind], recv_sem=recv_sem.at[index],
+            device_id=dev, device_id_type=MESH,
+        )
+
+    def pair_copy(index, kind, dev):
+        return pltpu.make_async_remote_copy(
+            src_ref=pairs.at[index], dst_ref=pairs.at[index], send_sem=pair_send.at[index, kind],
+            recv_sem=pair_recv.at[index], device_id=dev, device_id_type=MESH,
+        )
+
+    sent = []
+
+    def send(index, kind, dev, source=None, when=None):
+        text = text_copy(index, kind, dev, buf.at[index] if source is None else source)
+        pair = pair_copy(index, kind, dev)
+
+        def begin():
+            text.start()
+            pair.start()
+
+        def finish():
+            text.wait_send()
+            pair.wait_send()
+
+        if when is None:
+            begin()
+            sent.append(finish)
+        else:
+            pl.when(when)(begin)
+            sent.append(lambda: pl.when(when)(finish))
+
+    def arrive(index):
+        text_copy(index, 0, dev_a, buf.at[index]).wait_recv()
+        pair_copy(index, 0, dev_a).wait_recv()
+
+    def column(k):
+        o = planes[k]
+        index = slot(o, n, w)
+        if k > 0:
+            arrive(index)
+        source = texts_ref if k == 0 else None
+        send(index, 3, dev_up, source, (o <= b) & (b < nb - 1))
+        send(index, 4, dev_down, source, (o >= b) & (b > 0))
+        send(index, 0, dev_a, source)
+        send(index, 1, dev_b, source)
+        send(index, 2, dev_p, source)
+
+    def from_a(k):
+        index = slot(planes[k], n_a, w_a)
+        arrive(index)
+        send(index, 1, dev_b)
+        send(index, 2, dev_p)
+
+    def from_b(k):
+        index = slot(planes[k], n_b, w_b)
+        arrive(index)
+        send(index, 2, dev_p)
+
+    def diagonal(k):
+        index = slot(planes[k], n_d, w_d)
+        arrive(index)
+        send(index, 2, dev_p)
+
+    def from_partner(k):
+        for nn_ in range(nn):
+            for half in range(nw // 2):
+                arrive(slot(planes[k], nn_, 2 * half + 1 - core))
+
+    column(0)
+
+    copy_rows.wait()
+    values = rows_ref[...].astype(F32)
+    mean = jnp.sum(values, axis=1, keepdims=True) / width
+    centered = values - mean
+    var = jnp.sum(centered * centered, axis=1, keepdims=True) / width
+    normed_ref[...] = (centered * lax.rsqrt(var + 1e-05) * gain_ref[...]).astype(BF16)
+
+    column(1)
+    from_a(0)
+    from_b(0)
+
+    weight_copy(w_d, 0, dev_x).wait_recv()
+    weight_copy(w_d, 2, dev_p).start()
+    weight_copy(w_p, 0, dev_x).wait_recv()
+    weight_copy(w_d + 1 - 2 * core, 0, dev_x).wait_recv()
+
+    for s in range(nw):
+        for k in range(pair_count):
+            at = (s * pair_count + k) * lanes
+            inner = jnp.dot(
+                normed_ref[:, at : at + lanes], block_diagonal(wts[s, k]), preferred_element_type=F32
+            )
+            active_ref[:, at : at + lanes] = jax.nn.gelu(inner, approximate=True).astype(BF16)
+
+    column(2)
+    from_a(1)
+    from_b(1)
+
+    step = 2 * lanes
+    row_id = lax.broadcasted_iota(jnp.int32, (width, step), 0)
+
+    def permute(lo, hi):
+        @pl.loop(lo, hi)
+        def _(c):
+            at = pl.ds(pl.multiple_of(c * step, step), step)
+            chosen = jnp.where(row_id == perm_ref[:, at], 1.0, 0.0).astype(BF16)
+            permuted_ref[:, at] = jnp.dot(active_ref[...], chosen, preferred_element_type=F32).astype(BF16)
+
+    chunks = width // step
+    permute(0, chunks // 4)
+    diagonal(0)
+    for k in range(3, nb):
+        column(k)
+    permute(chunks // 4, chunks // 2)
+    from_a(2)
+    from_b(2)
+    permute(chunks // 2, chunks)
+    diagonal(1)
+
+    for s in range(nw):
+        for k in range(pair_count):
+            at = (s * pair_count + k) * lanes
+            outer = jnp.dot(
+                permuted_ref[:, at : at + lanes], block_diagonal(wts[s, pair_count + k]), preferred_element_type=F32
+            )
+            emb_ref[:, at : at + lanes] = (rows_ref[:, at : at + lanes].astype(F32) + outer).astype(BF16)
+
+    logit_scale = LOGIT_GAIN / math.sqrt(width)
+    copy_text.wait()
+
+    def scores(k):
+        from_partner(k)
+        block = buf[pl.ds(planes[k] * group, group)].reshape(group * t_rows, width)
+        product = lax.dot_general(emb_ref[...], block, (((1,), (1,)), ((), ())), preferred_element_type=F32)
+        score_ref[planes[k]] = product * logit_scale
+
+    for k in range(3, nb):
+        from_a(k)
+        from_b(k)
+    scores(0)
+    diagonal(2)
+    scores(1)
+    for k in range(3, nb):
+        diagonal(k)
+    for k in range(2, nb):
+        scores(k)
+
+    columns = group * t_rows
+    total_rows = img_pair_ref.shape[1]
+    place = lax.broadcasted_iota(jnp.int32, (r_rows, total_rows), 1) == (
+        lax.broadcasted_iota(jnp.int32, (r_rows, total_rows), 0) + me * r_rows
+    )
+    own_ids = jnp.sum(jnp.where(place, img_pair_ref[...], 0), axis=1, keepdims=True)
+    quarter = lax.broadcasted_iota(jnp.int32, (1, nw * t_rows), 1) // t_rows
+
+    def pair_row(first):
+        row = pairs[first]
+        for ww_ in range(1, nw):
+            row = jnp.where(quarter == ww_, pairs[first + ww_], row)
+        return row
+
+    found = [
+        own_ids == jnp.concatenate([pair_row(slot(o, nn_, 0)) for nn_ in range(nn)], axis=1) for o in range(nb)
+    ]
+    parts = [score_ref[o] for o in range(nb)]
+    row_max = functools.reduce(jnp.maximum, [jnp.max(part, axis=1, keepdims=True) for part in parts])
+    shifted = [jnp.exp(part - row_max) for part in parts]
+    totals = functools.reduce(jnp.add, [jnp.sum(part, axis=1, keepdims=True) for part in shifted])
+    positive = functools.reduce(
+        jnp.add, [jnp.sum(jnp.where(hit, part, 0.0), axis=1, keepdims=True) for hit, part in zip(found, parts)]
+    )
+    row_loss = row_max + jnp.log(totals) - positive
+    losses[me] = jnp.sum(jnp.where(place, row_loss, 0.0), axis=0, keepdims=True)
+    dscore = [
+        (part / totals - jnp.where(hit, 1.0, 0.0)).astype(BF16) for hit, part in zip(found, shifted)
+    ]
+
+    tile = width // 4
+
+    def gradient(c):
+        at = slice(c * tile, (c + 1) * tile)
+        total = jnp.zeros((r_rows, tile), F32)
+        for o in range(nb):
+            block = buf[o * group : (o + 1) * group, :, at].reshape(columns, tile)
+            total = total + jnp.dot(dscore[o], block, preferred_element_type=F32)
+        grad_ref[:, at] = total.astype(BF16)
+
+    gradient(0)
+    loss_copies = []
+    for position, dev in enumerate(near):
+        loss_copies.append(
+            pltpu.make_async_remote_copy(
+                src_ref=losses.at[me], dst_ref=losses.at[me], send_sem=loss_send.at[position],
+                recv_sem=loss_recv.at[me], device_id=dev, device_id_type=MESH,
+            )
+        )
+        loss_copies[-1].start()
+    for c in range(1, 4):
+        gradient(c)
+    for _, n_o, w_o in near:
+        other = n_o * nw + w_o
+        pltpu.make_async_remote_copy(
+            src_ref=losses.at[other], dst_ref=losses.at[other], send_sem=loss_send.at[0],
+            recv_sem=loss_recv.at[other], device_id=dev_p, device_id_type=MESH,
+        ).wait_recv()
+    loss_ref[...] = functools.reduce(jnp.add, [losses[i] for i in range(group)])
+
+    for finish in sent:
+        finish()
+    weight_copy(w, 0, dev_x).wait_send()
+    weight_copy(w, 1, dev_p).wait_send()
+    weight_copy(w_d, 2, dev_p).wait_send()
+    for copy in loss_copies:
+        copy.wait_send()
+
+
+def fused(dims, images, img_pair, texts, txt_pair, gain, perm, right_blocks, left_blocks):
+    nb, nn, nw = dims
+    group = nn * nw
+    devices = nb * group
+    t_rows, width = texts.shape
+    r_rows = images.shape[0] // group
+    block_count, size = right_blocks.shape[:2]
+    vmem = pl.BlockSpec(memory_space=pltpu.VMEM)
+    hbm = pl.BlockSpec(memory_space=pl.ANY)
+    dma = pltpu.SemaphoreType.DMA
+    grad, loss = pl.pallas_call(
+        functools.partial(fused_kernel, dims),
+        out_shape=(
+            jax.ShapeDtypeStruct((r_rows, width), BF16),
+            jax.ShapeDtypeStruct((1, images.shape[0]), F32),
+        ),
+        in_specs=[hbm, vmem, hbm, vmem, vmem, vmem, vmem, vmem],
+        out_specs=(vmem, vmem),
+        scratch_shapes=[
+            pltpu.VMEM((r_rows, width), BF16),
+            pltpu.VMEM((nw, block_count, size, 2 * size), BF16),
+            pltpu.VMEM((devices, t_rows, width), BF16),
+            pltpu.VMEM((devices, 1, nw * t_rows), jnp.int32),
+            pltpu.VMEM((r_rows, width), BF16),
+            pltpu.VMEM((r_rows, width), BF16),
+            pltpu.VMEM((r_rows, width), BF16),
+            pltpu.VMEM((r_rows, width), BF16),
+            pltpu.VMEM((nb, r_rows, group * t_rows), F32),
+            pltpu.VMEM((group, 1, images.shape[0]), F32),
+            dma((2,)),
+            dma((3,)),
+            dma((nw,)),
+            dma((devices, 5)),
+            dma((devices,)),
+            dma((devices, 5)),
+            dma((devices,)),
+            dma((group - 1,)),
+            dma((group,)),
+        ],
+        compiler_params=pltpu.CompilerParams(
+            collective_id=0, has_side_effects=True, vmem_limit_bytes=48 * 2**20
+        ),
+    )(
+        images, img_pair[None], texts, txt_pair[None], gain[None], perm[None], right_blocks, left_blocks
+    )
+    return grad, loss[0]
 
 
 def monarch(images, gain, perm, right_full, left_full):
@@ -69,8 +431,17 @@
 
 
 def solution(mesh):
+    dims = tuple(mesh.shape[axis] for axis in ("batch", "neg", "weight"))
+
+    def body(images, img_pair, texts, txt_pair, gain, perm, right_blocks, left_blocks):
+        args = (images, img_pair, texts, txt_pair, gain, perm, right_blocks, left_blocks)
+        text_bytes = math.prod(dims) * texts.size * texts.dtype.itemsize
+        if dims[1:] == (2, 4) and dims[0] >= 3 and text_bytes <= VMEM_FOR_TEXTS:
+            return fused(dims, *args)
+        return per_device(*args)
+
     return jax.shard_map(
-        per_device,
+        body,
         mesh=mesh,
         in_specs=(
             P("batch", None),

time: 140 us -> 49.5 us (0.35)
  blocking collectives: 64.6 us -> 0 us
  Pallas kernels: 0 us -> 41.3 us
  waiting for transfers between devices: 39.5 us -> 0 us
  between operations: 14.8 us -> 0.66 us
  matrix products: 5.03 us -> 0 us
  other arithmetic: 4.98 us -> 0 us
  local copies, waits for them, and re-layouts: 10.6 us -> 7.22 us
    pallas_call x0 -> x1, Pallas kernels: none -> 41.3 us  [fused(): pl.pallas_call(functools.partial(fused_kernel, dims), out_shape=(jax.Shap...]
    reduce_scatter x1 -> x0, waiting for transfers between devices: 39.5 us -> none  [per_device(): lax.psum_scatter(jnp.dot(dscore, gathered, preferred_element_type=jnp.flo...]
    all_gather x3 -> x0, blocking collectives: 32.8 us -> none  [the longest x1 16.5 us: per_device(): lax.all_gather(texts, 'batch', axis=0, tiled=True)]
    pmax x1 -> x0, blocking collectives: 12.3 us -> none  [per_device(): row_max = lax.pmax(local_max, ('neg', 'weight'))]
    psum x1 -> x0, blocking collectives: 11.8 us -> none  [per_device(): lax.psum((jnp.sum(shifted, axis=1), local_pos), ('neg', 'weight'))]
    unnamed x1 -> x0, blocking collectives: 7.67 us -> none
    gather x1 -> x0, local copies, waits for them, and re-layouts: 7.5 us -> none  [monarch(): permuted = jnp.take(active, perm, axis=1)]
    dot_general x4 -> x0, matrix products: 5.03 us -> none  [the longest x1 1.91 us: monarch(): jnp.einsum('rke,kec->rkc', permuted.reshape(row_count, block_count, block...]
  transfers between devices with their start and end apart: 1 -> 0, of which waited for: 1 -> 0; matrix products, arithmetic and copies ran while one was open for 0% -> 0% of each run, Pallas kernels for 0% -> 0%
where the time goes in v1:
time: 49.5 us; the launch traced here: 49.2 us
  Pallas kernels  41.3 us (83%)
  local copies, waits for them, and re-layouts  7.22 us (15%)
  between operations  0.66 us (1%)
    pallas_call x1, Pallas kernels, fused(): pl.pallas_call(functools.partial(fused_kernel, dims), out_shape=(jax.Shap...  41.3 us
    unnamed x18, local copies, waits for them, and re-layouts  7.22 us

profile of v1, /device:TPU:0, one launch (start us, length us, event | category | flops | bytes accessed | tf_op | source)
XLA Modules:
  0.0 49.2 jit_solution(3091016516387748358)
XLA Ops:
  0.6 0.0 copy-start.6
  0.6 0.0 copy-start.7
  0.7 0.7 %copy-done.6 = s32[256]{0:T(256)S(1)} copy-done((s32[256]{0:T(256)S(1)}, s32[256]{0:T(256)}, u32[]{:S(2)}) %copy-start.6) | copy-done | bytes 1048
  1.3 0.0 copy-done.7
  1.3 0.0 copy-start
  1.3 1.2 %copy-done = bf16[256,2048]{1,0:T(8,128)(2,1)S(1)} copy-done((bf16[256,2048]{1,0:T(8,128)(2,1)S(1)}, bf16[256,2048]{1,0:T(8,128)(2,1)}, u32[]{:S(2)}) %copy-start) | copy-done | bytes 1048600
  2.5 0.0 copy-start.1
  2.5 0.9 %copy-done.1 = bf16[32,2048]{1,0:T(8,128)(2,1)S(1)} copy-done((bf16[32,2048]{1,0:T(8,128)(2,1)S(1)}, bf16[32,2048]{1,0:T(8,128)(2,1)}, u32[]{:S(2)}) %copy-start.1) | copy-done | bytes 131096
  3.4 0.0 copy-start.2
  3.4 0.9 %copy-done.2 = bf16[8,64,64]{2,1,0:T(8,128)(2,1)S(1)} copy-done((bf16[8,64,64]{2,1,0:T(8,128)(2,1)S(1)}, bf16[8,64,64]{2,1,0:T(8,128)(2,1)}, u32[]{:S(2)}) %copy-start.2) | copy-done | bytes 65560
  4.4 0.0 copy-start.3
  4.4 0.9 %copy-done.3 = bf16[8,64,64]{2,1,0:T(8,128)(2,1)S(1)} copy-done((bf16[8,64,64]{2,1,0:T(8,128)(2,1)S(1)}, bf16[8,64,64]{2,1,0:T(8,128)(2,1)}, u32[]{:S(2)}) %copy-start.3) | copy-done | bytes 65560
  5.3 0.0 copy-start.4
  5.3 0.7 %copy-done.4 = f32[2048]{0:T(1024)S(1)} copy-done((f32[2048]{0:T(1024)S(1)}, f32[2048]{0:T(1024)}, u32[]{:S(2)}) %copy-start.4) | copy-done | bytes 8216
  6.0 0.0 copy-start.5
  6.0 0.7 %copy-done.5 = s32[2048]{0:T(1024)S(1)} copy-done((s32[2048]{0:T(1024)S(1)}, s32[2048]{0:T(1024)}, u32[]{:S(2)}) %copy-start.5) | copy-done | bytes 8216
  6.7 41.3 %shard_map.95 = (bf16[32,2048]{1,0:T(8,128)(2,1)S(1)}, f32[1,256]{1,0:T(1,128)S(1)}) custom-call(bf16[256,2048]{1,0:T(8,128)(2,1)S(1)} %copy-done, s32[1,256]{1,0:T(1,128)S(1)} %bitcast.7, bf16[32,2048]{1,0:T(8,128)(2,1)S(1)} %copy-done.1, s32[1,32]{1,0:T(1,128)S(1)} %bitcast.9, f32[1,2048]{1,0:T(1,128)S(1)} %bitcast.5, s32[1,2048]{1,0:T(1,128)S(1)} %bitcast.6, ...), custom_call_target="tpu_custom_call" | custom-call | tf_op jit(solution)/shard_map/pallas_call | solution.py:335
  48.0 0.7 %copy.12 = bf16[32,2048]{1,0:T(8,128)(2,1)} copy(bf16[32,2048]{1,0:T(8,128)(2,1)S(1)} %get-tuple-element.8) | data formatting | bytes 262144
  48.6 0.6 %copy.13 = f32[256]{0:T(256)} copy(f32[256]{0:T(256)S(1)} %bitcast.8) | data formatting | bytes 2048
Async XLA Ops:
  0.6 0.7 %copy-start.6 = (s32[256]{0:T(256)S(1)}, s32[256]{0:T(256)}, u32[]{:S(2)}) copy-start(s32[256]{0:T(256)} %param.9) | copy-start | bytes 3076
  0.6 0.7 %copy-start.7 = (s32[32]{0:T(128)S(1)}, s32[32]{0:T(128)}, u32[]{:S(2)}) copy-start(s32[32]{0:T(128)} %param.11) | copy-start | bytes 388
  1.3 1.2 %copy-start = (bf16[256,2048]{1,0:T(8,128)(2,1)S(1)}, bf16[256,2048]{1,0:T(8,128)(2,1)}, u32[]{:S(2)}) copy-start(bf16[256,2048]{1,0:T(8,128)(2,1)} %images_ref.1) | copy-start | bytes 3145732
  2.5 0.9 %copy-start.1 = (bf16[32,2048]{1,0:T(8,128)(2,1)S(1)}, bf16[32,2048]{1,0:T(8,128)(2,1)}, u32[]{:S(2)}) copy-start(bf16[32,2048]{1,0:T(8,128)(2,1)} %texts_ref.1) | copy-start | bytes 393220
  3.4 0.9 %copy-start.2 = (bf16[8,64,64]{2,1,0:T(8,128)(2,1)S(1)}, bf16[8,64,64]{2,1,0:T(8,128)(2,1)}, u32[]{:S(2)}) copy-start(bf16[8,64,64]{2,1,0:T(8,128)(2,1)} %right_ref.1) | copy-start | bytes 196612
  4.4 0.9 %copy-start.3 = (bf16[8,64,64]{2,1,0:T(8,128)(2,1)S(1)}, bf16[8,64,64]{2,1,0:T(8,128)(2,1)}, u32[]{:S(2)}) copy-start(bf16[8,64,64]{2,1,0:T(8,128)(2,1)} %left_ref.1) | copy-start | bytes 196612
  5.3 0.7 %copy-start.4 = (f32[2048]{0:T(1024)S(1)}, f32[2048]{0:T(1024)}, u32[]{:S(2)}) copy-start(f32[2048]{0:T(1024)} %param.12) | copy-start | bytes 24580
  6.0 0.7 %copy-start.5 = (s32[2048]{0:T(1024)S(1)}, s32[2048]{0:T(1024)}, u32[]{:S(2)}) copy-start(s32[2048]{0:T(1024)} %param.13) | copy-start | bytes 24580

commit v2 on v1

--- a/solution.py
+++ b/solution.py
@@ -11,6 +11,7 @@
 LOGIT_GAIN = 2.8
 MESH = pl.DeviceIdType.MESH
 F32, BF16 = jnp.float32, jnp.bfloat16
+PARTS = 1
 VMEM_FOR_TEXTS = 16 * 2**20
 
 
@@ -28,8 +29,8 @@
 
 
 def fused_kernel(
-    dims, images_ref, img_pair_ref, texts_ref, txt_pair_ref, gain_ref, perm_ref, right_ref, left_ref,
-    grad_ref, loss_ref,
+    dims, images_hbm, img_pair_hbm, texts_ref, txt_pair_hbm, gain_hbm, perm_hbm, right_hbm, left_hbm,
+    grad_ref, loss_ref, img_pair_ref, txt_pair_ref, gain_ref, perm_ref, right_ref, left_ref,
     rows_ref, wts, buf, pairs, normed_ref, active_ref, permuted_ref, emb_ref, score_ref, losses,
     local_sem, wt_send, wt_recv, send_sem, recv_sem, pair_send, pair_recv, loss_send, loss_recv,
 ):
@@ -67,17 +68,6 @@
 
     planes = [origin(k) for k in range(nb)]
 
-    own_slot = slot(b, n, w)
-    copy_rows = pltpu.make_async_copy(images_ref.at[pl.ds(pl.multiple_of(me * r_rows, r_rows), r_rows)], rows_ref, local_sem.at[0])
-    copy_text = pltpu.make_async_copy(texts_ref, buf.at[own_slot], local_sem.at[1])
-    copy_rows.start()
-    copy_text.start()
-    for k in range(pair_count):
-        wts[w, k] = jnp.concatenate([right_ref[2 * k], right_ref[2 * k + 1]], axis=1)
-        wts[w, pair_count + k] = jnp.concatenate([left_ref[2 * k], left_ref[2 * k + 1]], axis=1)
-    ids = txt_pair_ref[...]
-    pairs[own_slot] = jnp.concatenate([ids] * nw, axis=1)
-
     barrier = pltpu.get_barrier_semaphore()
     near = [dev_a, dev_b, dev_p, (b, n_d, w_d)]
     near += [(b, n_a, w_a + 1 - 2 * core), (b, n_b, w_b + 1 - 2 * core), (b, n_d, w_d + 1 - 2 * core)]
@@ -92,6 +82,20 @@
     def _():
         pl.semaphore_signal(barrier, inc=1, device_id=dev_down, device_id_type=MESH)
 
+    own_slot = slot(b, n, w)
+    staged = [
+        pltpu.make_async_copy(source, target, local_sem.at[2 + i])
+        for i, (source, target) in enumerate([
+            (right_hbm, right_ref), (left_hbm, left_ref), (txt_pair_hbm, txt_pair_ref),
+            (gain_hbm, gain_ref), (perm_hbm, perm_ref), (img_pair_hbm, img_pair_ref),
+        ])
+    ]
+    for copy in staged:
+        copy.start()
+    copy_rows = pltpu.make_async_copy(images_hbm.at[pl.ds(pl.multiple_of(me * r_rows, r_rows), r_rows)], rows_ref, local_sem.at[0])
+    copy_text = pltpu.make_async_copy(texts_ref, buf.at[own_slot], local_sem.at[1])
+    copy_rows.start()
+    copy_text.start()
     expected = len(near) + jnp.where(b < nb - 1, 1, 0) + jnp.where(b > 0, 1, 0)
     pl.semaphore_wait(barrier, expected)
 
@@ -101,13 +105,13 @@
             device_id=dev, device_id_type=MESH,
         )
 
-    weight_copy(w, 0, dev_x).start()
-    weight_copy(w, 1, dev_p).start()
-
-    def text_copy(index, kind, dev, source):
+    half = t_rows // PARTS
+
+    def text_copy(index, kind, part, dev, source):
+        rows = pl.ds(part * half, half)
         return pltpu.make_async_remote_copy(
-            src_ref=source, dst_ref=buf.at[index], send_sem=send_sem.at[index, kind], recv_sem=recv_sem.at[index],
-            device_id=dev, device_id_type=MESH,
+            src_ref=source.at[rows], dst_ref=buf.at[index, rows], send_sem=send_sem.at[index, kind, part],
+            recv_sem=recv_sem.at[index, part], device_id=dev, device_id_type=MESH,
         )
 
     def pair_copy(index, kind, dev):
@@ -118,79 +122,123 @@
 
     sent = []
 
-    def send(index, kind, dev, source=None, when=None):
-        text = text_copy(index, kind, dev, buf.at[index] if source is None else source)
-        pair = pair_copy(index, kind, dev)
-
-        def begin():
-            text.start()
-            pair.start()
-
-        def finish():
-            text.wait_send()
-            pair.wait_send()
-
+    def launch(copy, when):
         if when is None:
-            begin()
-            sent.append(finish)
+            copy.start()
+            sent.append(copy.wait_send)
         else:
-            pl.when(when)(begin)
-            sent.append(lambda: pl.when(when)(finish))
-
-    def arrive(index):
-        text_copy(index, 0, dev_a, buf.at[index]).wait_recv()
-        pair_copy(index, 0, dev_a).wait_recv()
+            pl.when(when)(copy.start)
+            sent.append(lambda: pl.when(when)(copy.wait_send))
+
+    def send_text(index, kind, part, dev, source, when):
+        launch(text_copy(index, kind, part, dev, source), when)
+
+    def send_pair(index, kind, dev, when):
+        launch(pair_copy(index, kind, dev), when)
+
+    def send(index, kind, part, dev, when=None):
+        send_text(index, kind, part, dev, buf.at[index], when)
+        if part == PARTS - 1:
+            send_pair(index, kind, dev, when)
+
+    def arrive(index, part):
+        text_copy(index, 0, part, dev_a, buf.at[index]).wait_recv()
+        if part == PARTS - 1:
+            pair_copy(index, 0, dev_a).wait_recv()
+
+    def along_chain(o, receiver):
+        distance = jnp.abs(o - receiver)
+        return distance < 0
 
     def column(k):
         o = planes[k]
         index = slot(o, n, w)
-        if k > 0:
-            arrive(index)
-        source = texts_ref if k == 0 else None
-        send(index, 3, dev_up, source, (o <= b) & (b < nb - 1))
-        send(index, 4, dev_down, source, (o >= b) & (b > 0))
-        send(index, 0, dev_a, source)
-        send(index, 1, dev_b, source)
-        send(index, 2, dev_p, source)
+        for part in range(PARTS):
+            arrive(index, part)
+            send(index, 3, part, dev_up, (o <= b) & (b < nb - 1))
+            send(index, 4, part, dev_down, (o >= b) & (b > 0))
+            send(index, 0, part, dev_a)
+            send(index, 1, part, dev_b)
+            send(index, 2, part, dev_p)
 
     def from_a(k):
         index = slot(planes[k], n_a, w_a)
-        arrive(index)
-        send(index, 1, dev_b)
-        send(index, 2, dev_p)
+        for part in range(PARTS):
+            arrive(index, part)
+            send(index, 1, part, dev_b, jnp.logical_not(along_chain(planes[k], b)) if k else None)
+            send(index, 2, part, dev_p)
 
     def from_b(k):
         index = slot(planes[k], n_b, w_b)
-        arrive(index)
-        send(index, 2, dev_p)
+        for part in range(PARTS):
+            arrive(index, part)
+            send(index, 2, part, dev_p)
 
     def diagonal(k):
-        index = slot(planes[k], n_d, w_d)
-        arrive(index)
-        send(index, 2, dev_p)
+        o = planes[k]
+        index = slot(o, n_d, w_d)
+        for part in range(PARTS):
+            arrive(index, part)
+            send(index, 3, part, dev_up, (o <= b) & (b < nb - 1) & along_chain(o, b + 1))
+            send(index, 4, part, dev_down, (o >= b) & (b > 0) & along_chain(o, b - 1))
+            send(index, 2, part, dev_p)
 
     def from_partner(k):
         for nn_ in range(nn):
-            for half in range(nw // 2):
-                arrive(slot(planes[k], nn_, 2 * half + 1 - core))
-
-    column(0)
-
-    copy_rows.wait()
-    values = rows_ref[...].astype(F32)
-    mean = jnp.sum(values, axis=1, keepdims=True) / width
-    centered = values - mean
-    var = jnp.sum(centered * centered, axis=1, keepdims=True) / width
-    normed_ref[...] = (centered * lax.rsqrt(var + 1e-05) * gain_ref[...]).astype(BF16)
+            for ww_ in range(nw // 2):
+                for part in range(PARTS):
+                    arrive(slot(planes[k], nn_, 2 * ww_ + 1 - core), part)
+
+    own_targets = [
+        (3, dev_up, b < nb - 1), (4, dev_down, b > 0), (0, dev_a, None), (1, dev_b, None), (2, dev_p, None),
+    ]
+
+    def own_sends(part):
+        for kind, dev, when in own_targets:
+            send_text(own_slot, kind, part, dev, texts_ref, when)
+
+    def layer_norm():
+        copy_rows.wait()
+        for copy in staged[3:]:
+            copy.wait()
+        values = rows_ref[...].astype(F32)
+        mean = jnp.sum(values, axis=1, keepdims=True) / width
+        centered = values - mean
+        var = jnp.sum(centered * centered, axis=1, keepdims=True) / width
+        normed_ref[...] = (centered * lax.rsqrt(var + 1e-05) * gain_ref[...]).astype(BF16)
+
+    for part in range(PARTS):
+        own_sends(part)
+
+    for copy in staged[:3]:
+        copy.wait()
+    ids = txt_pair_ref[...]
+    pairs[own_slot] = jnp.concatenate([ids] * nw, axis=1)
+    for k in range(pair_count):
+        wts[w, k] = jnp.concatenate([right_ref[2 * k], right_ref[2 * k + 1]], axis=1)
+        wts[w, pair_count + k] = jnp.concatenate([left_ref[2 * k], left_ref[2 * k + 1]], axis=1)
+    layer_norm()
+    for kind, dev, when in own_targets:
+        send_pair(own_slot, kind, dev, when)
+    weight_copy(w, 0, dev_x).start()
+    weight_copy(w, 1, dev_p).start()
 
     column(1)
     from_a(0)
     from_b(0)
-
+    column(2)
+    from_a(1)
     weight_copy(w_d, 0, dev_x).wait_recv()
     weight_copy(w_d, 2, dev_p).start()
+    for k in range(3, nb):
+        column(k)
+    diagonal(0)
+    from_b(1)
+    from_a(2)
     weight_copy(w_p, 0, dev_x).wait_recv()
     weight_copy(w_d + 1 - 2 * core, 0, dev_x).wait_recv()
+    diagonal(1)
+    from_b(2)
 
     for s in range(nw):
         for k in range(pair_count):
@@ -200,10 +248,6 @@
             )
             active_ref[:, at : at + lanes] = jax.nn.gelu(inner, approximate=True).astype(BF16)
 
-    column(2)
-    from_a(1)
-    from_b(1)
-
     step = 2 * lanes
     row_id = lax.broadcasted_iota(jnp.int32, (width, step), 0)
 
@@ -215,15 +259,12 @@
             permuted_ref[:, at] = jnp.dot(active_ref[...], chosen, preferred_element_type=F32).astype(BF16)
 
     chunks = width // step
-    permute(0, chunks // 4)
-    diagonal(0)
     for k in range(3, nb):
-        column(k)
-    permute(chunks // 4, chunks // 2)
-    from_a(2)
-    from_b(2)
+        from_a(k)
+    permute(0, chunks // 2)
+    for k in range(3, nb):
+        from_b(k)
     permute(chunks // 2, chunks)
-    diagonal(1)
 
     for s in range(nw):
         for k in range(pair_count):
@@ -242,9 +283,6 @@
         product = lax.dot_general(emb_ref[...], block, (((1,), (1,)), ((), ())), preferred_element_type=F32)
         score_ref[planes[k]] = product * logit_scale
 
-    for k in range(3, nb):
-        from_a(k)
-        from_b(k)
     scores(0)
     diagonal(2)
     scores(1)
@@ -283,7 +321,7 @@
         (part / totals - jnp.where(hit, 1.0, 0.0)).astype(BF16) for hit, part in zip(found, shifted)
     ]
 
-    tile = width // 4
+    tile = width // 8
 
     def gradient(c):
         at = slice(c * tile, (c + 1) * tile)
@@ -303,7 +341,7 @@
             )
         )
         loss_copies[-1].start()
-    for c in range(1, 4):
+    for c in range(1, 8):
         gradient(c)
     for _, n_o, w_o in near:
         other = n_o * nw + w_o
@@ -330,7 +368,7 @@
     r_rows = images.shape[0] // group
     block_count, size = right_blocks.shape[:2]
     vmem = pl.BlockSpec(memory_space=pltpu.VMEM)
-    hbm = pl.BlockSpec(memory_space=pl.ANY)
+    hbm = pl.BlockSpec(memory_space=pltpu.HBM)
     dma = pltpu.SemaphoreType.DMA
     grad, loss = pl.pallas_call(
         functools.partial(fused_kernel, dims),
@@ -338,9 +376,15 @@
             jax.ShapeDtypeStruct((r_rows, width), BF16),
             jax.ShapeDtypeStruct((1, images.shape[0]), F32),
         ),
-        in_specs=[hbm, vmem, hbm, vmem, vmem, vmem, vmem, vmem],
+        in_specs=[hbm] * 8,
         out_specs=(vmem, vmem),
         scratch_shapes=[
+            pltpu.VMEM((1, images.shape[0]), jnp.int32),
+            pltpu.VMEM((1, t_rows), jnp.int32),
+            pltpu.VMEM((1, width), F32),
+            pltpu.VMEM((1, width), jnp.int32),
+            pltpu.VMEM(right_blocks.shape, BF16),
+            pltpu.VMEM(left_blocks.shape, BF16),
             pltpu.VMEM((r_rows, width), BF16),
             pltpu.VMEM((nw, block_count, size, 2 * size), BF16),
             pltpu.VMEM((devices, t_rows, width), BF16),
@@ -351,18 +395,18 @@
             pltpu.VMEM((r_rows, width), BF16),
             pltpu.VMEM((nb, r_rows, group * t_rows), F32),
             pltpu.VMEM((group, 1, images.shape[0]), F32),
-            dma((2,)),
+            dma((8,)),
             dma((3,)),
             dma((nw,)),
-            dma((devices, 5)),
-            dma((devices,)),
+            dma((devices, 5, PARTS)),
+            dma((devices, PARTS)),
             dma((devices, 5)),
             dma((devices,)),
             dma((group - 1,)),
             dma((group,)),
         ],
         compiler_params=pltpu.CompilerParams(
-            collective_id=0, has_side_effects=True, vmem_limit_bytes=48 * 2**20
+            collective_id=0, has_side_effects=True, vmem_limit_bytes=67_043_328
         ),
     )(
         images, img_pair[None], texts, txt_pair[None], gain[None], perm[None], right_blocks, left_blocks
@@ -436,7 +480,7 @@
     def body(images, img_pair, texts, txt_pair, gain, perm, right_blocks, left_blocks):
         args = (images, img_pair, texts, txt_pair, gain, perm, right_blocks, left_blocks)
         text_bytes = math.prod(dims) * texts.size * texts.dtype.itemsize
-        if dims[1:] == (2, 4) and dims[0] >= 3 and text_bytes <= VMEM_FOR_TEXTS:
+        if dims[1:] == (2, 4) and dims[0] >= 3 and texts.shape[0] % (16 * PARTS) == 0 and text_bytes <= VMEM_FOR_TEXTS:
             return fused(dims, *args)
         return per_device(*args)
 

time: 49.5 us -> 41.5 us (0.84)
  local copies, waits for them, and re-layouts: 7.22 us -> 2.14 us
  Pallas kernels: 41.3 us -> 38.5 us
    unnamed x18 -> x4, local copies, waits for them, and re-layouts: 7.22 us -> 2.14 us
    pallas_call x1, Pallas kernels: 41.3 us -> 38.5 us  [fused(): pl.pallas_call(functools.partial(fused_kernel, dims), out_shape=(jax.Shap...]
where the time goes in v2:
time: 41.5 us; the launch traced here: 41.3 us
  Pallas kernels  38.5 us (93%)
  local copies, waits for them, and re-layouts  2.14 us (5%)
  between operations  0.65 us (2%)
    pallas_call x1, Pallas kernels, fused(): pl.pallas_call(functools.partial(fused_kernel, dims), out_shape=(jax.Shap...  38.5 us
    unnamed x4, local copies, waits for them, and re-layouts  2.14 us

profile of v2, /device:TPU:0, one launch (start us, length us, event | category | flops | bytes accessed | tf_op | source)
XLA Modules:
  0.0 41.3 jit_solution(1933072449511344607)
XLA Ops:
  0.6 38.5 %shard_map.95 = (bf16[32,2048]{1,0:T(8,128)(2,1)}, f32[1,256]{1,0:T(1,128)}) custom-call(bf16[256,2048]{1,0:T(8,128)(2,1)} %images_hbm.1, s32[1,256]{1,0:T(1,128)} %bitcast.7, bf16[32,2048]{1,0:T(8,128)(2,1)} %texts_ref.1, s32[1,32]{1,0:T(1,128)} %bitcast.9, f32[1,2048]{1,0:T(1,128)} %bitcast.5, s32[1,2048]{1,0:T(1,128)} %bitcast.6, ...), custom_call_target="tpu_custom_call" | custom-call | tf_op jit(solution)/shard_map/pallas_call | solution.py:373
  39.2 0.0 copy-start
  39.2 1.6 %copy.12 = bf16[32,2048]{1,0:T(8,128)(2,1)} copy(bf16[32,2048]{1,0:T(8,128)(2,1)} %get-tuple-element.8) | data formatting | bytes 262144
  40.8 0.0 copy-done
  40.8 0.6 %copy.13 = f32[256]{0:T(256)} copy(f32[256]{0:T(256)S(1)} %bitcast.8) | data formatting | bytes 2048
Async XLA Ops:
  39.2 1.6 %copy-start = (f32[1,256]{1,0:T(1,128)S(1)}, f32[1,256]{1,0:T(1,128)}, u32[]{:S(2)}) copy-start(f32[1,256]{1,0:T(1,128)} %get-tuple-element.5) | copy-start | bytes 3076
